TPU v7x, 128 devices: a whole 4x4x4 slice. The times are simulated.
128 devices in a mesh: group: 16 (over z, y), inner: 8 (over x, core).
Axes of the slice: x: 4, y: 4, z: 4, core: 2. Of those that a mesh axis runs over, the one named last changes fastest.
Arguments:
- tokens: bfloat16 [16384, 7168], P(('group', 'inner')), may hold values from -6 to 6
- target: int32 [16384], P(('group', 'inner')), may hold values from 0 to 16, as said below
- gate_scale: float32 [16384], P(('group', 'inner')), may hold values from 0.25 to 2.5
- gate_weight: bfloat16 [16, 7168, 2048], P('group', None, 'inner'), may hold values from -0.0625 to 0.0625
- up_weight: bfloat16 [16, 7168, 2048], P('group', None, 'inner'), may hold values from -0.0625 to 0.0625
- down_weight: bfloat16 [16, 2048, 7168], P('group', 'inner'), may hold values from -0.125 to 0.125
Outputs:
- routed_out: bfloat16 [16384, 7168], P(('group', 'inner'))
Inputs may be any that keep to these rules, and one draw needn't show every extreme that they name: 16 means that the token uses no expert of this round. Among the 128 tokens of one device at most 10 target any one group, and in every device some group is targeted by exactly 10 of them.
All inputs are finite; a program needn't handle non-finite values.
Results may differ from a plain program's by a relative error of at most 0.0095.
Values may be sent and summed in bfloat16 or wider, within the bound.
A program may use at most 192 MiB of HBM per device.

v0:
```python
import jax
import jax.numpy as jnp
from jax import lax
from jax.sharding import PartitionSpec as P


def expert_part(rows_in, gate_mat, up_mat, down_mat):
    gate_pre = jnp.dot(rows_in, gate_mat, preferred_element_type=jnp.float32)
    up_pre = jnp.dot(rows_in, up_mat, preferred_element_type=jnp.float32)
    hidden = (jax.nn.silu(gate_pre) * up_pre).astype(jnp.bfloat16)
    return jnp.dot(hidden, down_mat, preferred_element_type=jnp.float32)


def body(tokens, target, gate_scale, gate_weight, up_weight, down_weight):
    groups = lax.axis_size("group")
    inner_size = lax.axis_size("inner")
    tok_count = tokens.shape[0]
    model_width = tokens.shape[1]
    capacity = tok_count * 5 // (4 * groups)
    slot_count = groups * capacity
    onehot = (target[:, None] == jnp.arange(groups, dtype=jnp.int32)[None, :]).astype(jnp.int32)
    rank_in = jnp.sum((jnp.cumsum(onehot, axis=0) - onehot) * onehot, axis=1)
    slot_of = jnp.where(target < groups, target * capacity + rank_in, slot_count)
    dispatch = (slot_of[None, :] == jnp.arange(slot_count, dtype=jnp.int32)[:, None]).astype(
        jnp.bfloat16
    )
    outbound = jnp.dot(dispatch, tokens, preferred_element_type=jnp.float32).astype(jnp.bfloat16)
    outbound = outbound.reshape(groups, capacity, model_width)
    received = lax.all_to_all(outbound, "group", 0, 0, tiled=True)
    gathered = lax.all_gather(received, "inner", axis=0, tiled=False)
    partial_value = expert_part(
        gathered.reshape(-1, model_width), gate_weight[0], up_weight[0], down_weight[0]
    )
    partial_value = partial_value.astype(jnp.bfloat16).reshape(
        inner_size, groups, capacity, model_width
    )
    pieces = lax.all_to_all(partial_value, "inner", 0, 0, tiled=True)
    summed = jnp.sum(pieces.astype(jnp.float32), axis=0).astype(jnp.bfloat16)
    back_rows = lax.all_to_all(summed, "group", 0, 0, tiled=True).reshape(slot_count, model_width)
    expert_out = lax.dot_general(
        dispatch, back_rows, (((0,), (0,)), ((), ())), preferred_element_type=jnp.float32
    )
    return (gate_scale[:, None] * expert_out).astype(jnp.bfloat16)


def solution(mesh):
    in_specs = (
        P(("group", "inner"), None),
        P(("group", "inner")),
        P(("group", "inner")),
        P("group", None, "inner"),
        P("group", None, "inner"),
        P("group", "inner", None),
    )
    out_specs = P(("group", "inner"), None)
    return jax.shard_map(body, mesh=mesh, in_specs=in_specs, out_specs=out_specs, check_vma=False)
```

profile of v0, /device:TPU:0, one launch (start us, length us, event | category | flops | bytes accessed | tf_op | source)
XLA Modules:
  0.0 581.5 jit_solution(12582657928746278648)
XLA Ops:
  6.5 0.0 copy-start
  6.5 0.9 fusion.18
  7.4 0.2 reduce_window_sum.11
  7.6 0.8 select_reduce_fusion
  8.4 0.7 compare_select_fusion
  9.1 2.1 convolution_convert_fusion.1
  11.2 4.5 reshape.15
  15.7 53.4 %all_to_all.15 = bf16[16,10,7168]{2,1,0:T(8,128)(2,1)S(1)} all-to-all(bf16[16,10,7168]{2,1,0:T(8,128)(2,1)} %reshape.15), channel_id=1, replica_groups=mesh['group'=16,'inner'=8] {'group'}, dimensions={0} | all-to-all | bytes 4587520 | tf_op jit(solution)/shard_map/all_to_all | solution.py:29
  69.1 2.6 copy.14
  71.7 0.0 all-gather.3.cloned.1.call-update
  71.7 89.1 %all-gather.3.cloned.1.call-done = bf16[128,10,7168]{2,0,1:T(8,128)(2,1)} async-done(((bf16[16,10,7168]{2,0,1:T(8,128)(2,1)}), bf16[128,10,7168]{2,0,1:T(8,128)(2,1)}) %all-gather.3.cloned.1.call-update) | async-done | bytes 18350096 | tf_op jit(solution)/shard_map/all_gather | solution.py:30
  160.9 21.5 %copy.15 = bf16[128,10,7168]{2,1,0:T(8,128)(2,1)} copy(bf16[128,10,7168]{2,0,1:T(8,128)(2,1)} %all-gather.3.cloned.1.call-done) | data formatting | bytes 36700160 | tf_op jit(solution)/shard_map/all_gather | solution.py:30
  182.4 28.2 %reshape.16 = bf16[1280,7168]{1,0:T(8,128)(2,1)} reshape(bf16[128,10,7168]{2,1,0:T(8,128)(2,1)} %copy.15) | data formatting | bytes 36700160 | tf_op jit(solution)/shard_map/reshape | solution.py:32
  210.6 9.8 %fusion.4 = f32[1280,256]{1,0:T(8,128)S(1)} fusion(bf16[1280,7168]{1,0:T(8,128)(2,1)} %reshape.16, bf16[1,7168,256]{2,1,0:T(8,128)(2,1)} %param.9), kind=kOutput, calls=%fused_computation.7 | convolution fusion | flops 4697620480 | bytes 23330816 | tf_op jit(solution)/shard_map/dot_general | solution.py:8
  220.4 27.1 %convolution_convert_fusion = bf16[1280,7168]{1,0:T(8,128)(2,1)} fusion(bf16[1,256,7168]{2,1,0:T(8,128)(2,1)} %param.11, bf16[1280,7168]{1,0:T(8,128)(2,1)} %reshape.16, bf16[1,7168,256]{2,1,0:T(8,128)(2,1)} %param.10, f32[1280,256]{1,0:T(8,128)S(1)} %fusion.4), kind=kOutput, calls=%fused_computation | convolution fusion | flops 9406382080 | bytes 45350912 | tf_op jit(solution)/shard_map/dot_general | solution.py:11
  247.6 27.7 %reshape.17 = bf16[8,16,10,7168]{3,2,1,0:T(8,128)(2,1)} reshape(bf16[1280,7168]{1,0:T(8,128)(2,1)} %convolution_convert_fusion) | data formatting | bytes 36700160 | tf_op jit(solution)/shard_map/reshape | solution.py:34
  275.2 17.2 %copy.16 = bf16[8,16,10,7168]{3,1,2,0:T(8,128)(2,1)S(1)} copy(bf16[8,16,10,7168]{3,2,1,0:T(8,128)(2,1)} %reshape.17) | data formatting | bytes 36700160 | tf_op jit(solution)/shard_map/reshape | solution.py:34
  292.4 208.1 %all_to_all.16 = bf16[8,16,10,7168]{3,1,2,0:T(8,128)(2,1)} all-to-all(bf16[8,16,10,7168]{3,1,2,0:T(8,128)(2,1)S(1)} %copy.16), channel_id=1, replica_groups=mesh['group'=16,'inner'=8] {'inner'}, dimensions={0} | all-to-all | bytes 36700160 | tf_op jit(solution)/shard_map/all_to_all | solution.py:37
  500.6 11.1 %reduce_sum.22 = bf16[16,10,7168]{2,0,1:T(8,128)(2,1)} reduce(bf16[8,16,10,7168]{3,1,2,0:T(8,128)(2,1)} %all_to_all.16, bf16[]{:T(256)} %constant.17.clone.1), dimensions={0}, to_apply=%region_2.3 | reduce | flops 8028160 | bytes 20643842 | tf_op jit(solution)/shard_map/reduce_sum | solution.py:38
  511.6 3.0 copy.17
  514.7 0.0 copy-start.1
  514.7 51.9 %all_to_all.17 = bf16[16,10,7168]{2,1,0:T(8,128)(2,1)} all-to-all(bf16[16,10,7168]{2,1,0:T(8,128)(2,1)S(1)} %copy.17), channel_id=1, replica_groups=mesh['group'=16,'inner'=8] {'group'}, dimensions={0} | all-to-all | bytes 4587520 | tf_op jit(solution)/shard_map/all_to_all | solution.py:39
  566.6 4.5 reshape.18
  571.1 3.6 fusion
  (5 shorter events, 0.0 us)
Async XLA Ops:
  6.5 2.6 copy-start
  6.5 154.3 %all-gather.3.cloned.1.call-start = ((), (), s32[]{:S(2)}) async-start(), calls=%async_computation.3 | async-start | bytes 20643840 | tf_op jit(solution)/shard_map/all_gather | solution.py:30
  514.7 60.0 %copy-start.1 = (bf16[128,7168]{1,0:T(8,128)(2,1)S(1)}, bf16[128,7168]{1,0:T(8,128)(2,1)}, u32[]{:S(2)}) copy-start(bf16[128,7168]{1,0:T(8,128)(2,1)} %param.6) | copy-start | bytes 5505028
  566.6 4.5 copy-start.2
Sparse Core Ops, SparseCore 0:
  71.9 88.9 all-gather.2
where the time goes:
time: 584 us; the launch traced here: 582 us
  blocking collectives  313 us (54%)
  local copies, waits for them, and re-layouts  109 us (19%)
  waiting for transfers between devices  89.2 us (15%)
  matrix products  42.7 us (7%)
  other arithmetic  13.6 us (2%)
  between operations  13.4 us (2%)
    all_to_all x1, blocking collectives, body(): pieces = lax.all_to_all(partial_value, 'inner', 0, 0, tiled=True)  208 us
    all_gather x1, waiting for transfers between devices, body(): gathered = lax.all_gather(received, 'inner', axis=0, tiled=False)  89.1 us
    all_to_all x1, blocking collectives, body(): received = lax.all_to_all(outbound, 'group', 0, 0, tiled=True)  53.4 us
    all_to_all x1, blocking collectives, body(): lax.all_to_all(summed, 'group', 0, 0, tiled=True)  51.9 us
    reshape x2, local copies, waits for them, and re-layouts, body(): partial_value.astype(jnp.bfloat16)  44.8 us
    reshape x1, local copies, waits for them, and re-layouts, body(): gathered.reshape(-1, model_width)  28.2 us
    dot_general x1, matrix products, expert_part(): return jnp.dot(hidden, down_mat, preferred_element_type=jnp.float32)  27.1 us
    all_gather x1, local copies, waits for them, and re-layouts, body(): gathered = lax.all_gather(received, 'inner', axis=0, tiled=False)  21.5 us
  transfers between devices with their start and end apart: 1, of which 1 were waited for; matrix products, arithmetic and copies ran while one was open for 0% of the time, Pallas kernels for 0%

commit v1 on v0

--- a/solution.py
+++ b/solution.py
@@ -2,6 +2,22 @@
 import jax.numpy as jnp
 from jax import lax
 from jax.sharding import PartitionSpec as P
+
+
+def exchange_in_pairs(x, axis, split, join):
+    ways, here = (lax.axis_size(axis), lax.axis_index(axis))
+    width = x.shape[split] // ways
+    dims = list(x.shape)
+    dims[split] = width
+    height = dims[join]
+    dims[join] = height * ways
+    full = jnp.zeros(dims, x.dtype)
+    for mask in range(ways):
+        part = lax.dynamic_slice_in_dim(x, (here ^ mask) * width, width, axis=split)
+        if mask:
+            part = lax.ppermute(part, axis, [(d, d ^ mask) for d in range(ways)])
+        full = lax.dynamic_update_slice_in_dim(full, part, (here ^ mask) * height, axis=join)
+    return full
 
 
 def expert_part(rows_in, gate_mat, up_mat, down_mat):
@@ -26,7 +42,7 @@
     )
     outbound = jnp.dot(dispatch, tokens, preferred_element_type=jnp.float32).astype(jnp.bfloat16)
     outbound = outbound.reshape(groups, capacity, model_width)
-    received = lax.all_to_all(outbound, "group", 0, 0, tiled=True)
+    received = exchange_in_pairs(outbound, "group", 0, 0)
     gathered = lax.all_gather(received, "inner", axis=0, tiled=False)
     partial_value = expert_part(
         gathered.reshape(-1, model_width), gate_weight[0], up_weight[0], down_weight[0]

time: 584 us -> 686 us (1.17)
  local copies, waits for them, and re-layouts: 109 us -> 193 us
  blocking collectives: 313 us -> 260 us
  waiting for transfers between devices: 89.2 us -> 129 us
  starting transfers between devices: 0.01 us -> 30.1 us
    dynamic_update_slice x0 -> x16, local copies, waits for them, and re-layouts: none -> 70.9 us  [exchange_in_pairs(): lax.dynamic_update_slice_in_dim(full, part, (here ^ mask) * height, axis=...]
    all_to_all x1 -> x0, blocking collectives: 53.4 us -> none  [body(): received = lax.all_to_all(outbound, 'group', 0, 0, tiled=True)]
    ppermute x0 -> x15, waiting for transfers between devices: none -> 37.6 us  [exchange_in_pairs(): part = lax.ppermute(part, axis, [(d, d ^ mask) for d in range(ways)])]
    ppermute x0 -> x15, starting transfers between devices: none -> 30.1 us  [exchange_in_pairs(): part = lax.ppermute(part, axis, [(d, d ^ mask) for d in range(ways)])]
    all_gather x1 -> x18, local copies, waits for them, and re-layouts: 21.5 us -> 32.6 us  [body(): gathered = lax.all_gather(received, 'inner', axis=0, tiled=False)]
  transfers between devices with their start and end apart: 1 -> 16, of which waited for: 1 -> 5; matrix products, arithmetic and copies ran while one was open for 0% -> 2% of each run, Pallas kernels for 0% -> 0%
where the time goes in v1:
time: 686 us; the launch traced here: 682 us
  blocking collectives  260 us (38%)
  local copies, waits for them, and re-layouts  193 us (28%)
  waiting for transfers between devices  129 us (19%)
  matrix products  42.9 us (6%)
  starting transfers between devices  30.1 us (4%)
  other arithmetic  13.6 us (2%)
  between operations  13.6 us (2%)
    all_to_all x1, blocking collectives, body(): pieces = lax.all_to_all(partial_value, 'inner', 0, 0, tiled=True)  208 us
    all_gather x1, waiting for transfers between devices, body(): gathered = lax.all_gather(received, 'inner', axis=0, tiled=False)  91.9 us
    dynamic_update_slice x16, local copies, waits for them, and re-layouts, exchange_in_pairs(): lax.dynamic_update_slice_in_dim(full, part, (here ^ mask) * height, axis=...  70.9 us
    all_to_all x1, blocking collectives, body(): lax.all_to_all(summed, 'group', 0, 0, tiled=True)  51.8 us
    reshape x2, local copies, waits for them, and re-layouts, body(): partial_value.astype(jnp.bfloat16)  44.9 us
    ppermute x15, waiting for transfers between devices, exchange_in_pairs(): part = lax.ppermute(part, axis, [(d, d ^ mask) for d in range(ways)])  37.6 us
    all_gather x18, local copies, waits for them, and re-layouts, body(): gathered = lax.all_gather(received, 'inner', axis=0, tiled=False)  32.6 us
    ppermute x15, starting transfers between devices, exchange_in_pairs(): part = lax.ppermute(part, axis, [(d, d ^ mask) for d in range(ways)])  30.1 us
  transfers between devices with their start and end apart: 16, of which 5 were waited for; matrix products, arithmetic and copies ran while one was open for 2% of the time, Pallas kernels for 0%

profile of v1, /device:TPU:0, one launch (start us, length us, event | category | flops | bytes accessed | tf_op | source)
XLA Modules:
  0.0 682.1 jit_solution(16055085075931606024)
XLA Ops:
  11.8 4.5 reshape.47
  19.6 6.6 collective-permute-start.14
  32.4 6.4 collective-permute-done.14
  48.2 18.1 %collective-permute-done.11 = bf16[1,10,7168]{2,1,0:T(8,128)(2,1)S(1)} collective-permute-done((bf16[1,10,7168]{2,1,0:T(8,128)(2,1)S(1)}, bf16[1,10,7168]{2,1,0:T(8,128)(2,1)S(1)}, u32[]{:S(2)}, u32[]{:S(2)}) %collective-permute-start.11) | collective-permute-done | bytes 143392 | tf_op jit(solution)/shard_map/ppermute | solution.py:18
  74.5 10.5 %collective-permute-done.6 = bf16[1,10,7168]{2,1,0:T(8,128)(2,1)S(1)} collective-permute-done((bf16[1,10,7168]{2,1,0:T(8,128)(2,1)S(1)}, bf16[1,10,7168]{2,1,0:T(8,128)(2,1)S(1)}, u32[]{:S(2)}, u32[]{:S(2)}) %collective-permute-start.6) | collective-permute-done | bytes 143392 | tf_op jit(solution)/shard_map/ppermute | solution.py:18
  89.1 4.4 dynamic_update_slice.64
  102.9 4.4 dynamic_update_slice.65
  107.3 4.4 dynamic_update_slice.66
  111.8 4.4 dynamic_update_slice.67
  116.2 4.4 dynamic_update_slice.68
  120.7 4.4 dynamic_update_slice.69
  125.1 4.4 dynamic_update_slice.70
  129.5 4.4 dynamic_update_slice.71
  169.4 91.9 %all-gather.2.cloned.1.call-done = bf16[8,16,10,7168]{3,1,2,0:T(8,128)(2,1)} async-done(((bf16[1,16,10,7168]{3,1,2,0:T(8,128)(2,1)}), bf16[8,16,10,7168]{3,1,2,0:T(8,128)(2,1)}) %all-gather.2.cloned.1.call-update) | async-done | bytes 18350096 | tf_op jit(solution)/shard_map/all_gather | solution.py:46
  261.3 21.5 %copy.77 = bf16[8,16,10,7168]{3,2,1,0:T(8,128)(2,1)} copy(bf16[8,16,10,7168]{3,1,2,0:T(8,128)(2,1)} %all-gather.2.cloned.1.call-done) | data formatting | bytes 36700160 | tf_op jit(solution)/shard_map/all_gather | solution.py:46
  282.7 28.3 %reshape.48 = bf16[1280,7168]{1,0:T(8,128)(2,1)} reshape(bf16[8,16,10,7168]{3,2,1,0:T(8,128)(2,1)} %copy.77) | data formatting | bytes 36700160 | tf_op jit(solution)/shard_map/reshape | solution.py:48
  311.0 9.8 %fusion.4 = f32[1280,256]{1,0:T(8,128)S(1)} fusion(bf16[1280,7168]{1,0:T(8,128)(2,1)} %reshape.48, bf16[1,7168,256]{2,1,0:T(8,128)(2,1)} %param.9), kind=kOutput, calls=%fused_computation.7 | convolution fusion | flops 4697620480 | bytes 23330816 | tf_op jit(solution)/shard_map/dot_general | solution.py:24
  320.8 27.4 %convolution_convert_fusion = bf16[1280,7168]{1,0:T(8,128)(2,1)} fusion(bf16[1,256,7168]{2,1,0:T(8,128)(2,1)} %param.11, bf16[1280,7168]{1,0:T(8,128)(2,1)} %reshape.48, bf16[1,7168,256]{2,1,0:T(8,128)(2,1)} %param.10, f32[1280,256]{1,0:T(8,128)S(1)} %fusion.4), kind=kOutput, calls=%fused_computation | convolution fusion | flops 9406382080 | bytes 45350912 | tf_op jit(solution)/shard_map/dot_general | solution.py:27
  348.2 27.7 %reshape.49 = bf16[8,16,10,7168]{3,2,1,0:T(8,128)(2,1)} reshape(bf16[1280,7168]{1,0:T(8,128)(2,1)} %convolution_convert_fusion) | data formatting | bytes 36700160 | tf_op jit(solution)/shard_map/reshape | solution.py:50
  375.9 17.2 %copy.78 = bf16[8,16,10,7168]{3,1,2,0:T(8,128)(2,1)S(1)} copy(bf16[8,16,10,7168]{3,2,1,0:T(8,128)(2,1)} %reshape.49) | data formatting | bytes 36700160 | tf_op jit(solution)/shard_map/reshape | solution.py:50
  393.1 208.2 %all_to_all.10 = bf16[8,16,10,7168]{3,1,2,0:T(8,128)(2,1)} all-to-all(bf16[8,16,10,7168]{3,1,2,0:T(8,128)(2,1)S(1)} %copy.78), channel_id=1, replica_groups=mesh['group'=16,'inner'=8] {'inner'}, dimensions={0} | all-to-all | bytes 36700160 | tf_op jit(solution)/shard_map/all_to_all | solution.py:53
  601.3 11.0 %reduce_sum.22 = bf16[16,10,7168]{2,0,1:T(8,128)(2,1)} reduce(bf16[8,16,10,7168]{3,1,2,0:T(8,128)(2,1)} %all_to_all.10, bf16[]{:T(256)} %constant.53.clone.1), dimensions={0}, to_apply=%region_2.3 | reduce | flops 8028160 | bytes 20643842 | tf_op jit(solution)/shard_map/reduce_sum | solution.py:54
  615.3 51.8 %all_to_all.11 = bf16[16,10,7168]{2,1,0:T(8,128)(2,1)} all-to-all(bf16[16,10,7168]{2,1,0:T(8,128)(2,1)S(1)} %copy.79), channel_id=1, replica_groups=mesh['group'=16,'inner'=8] {'group'}, dimensions={0} | all-to-all | bytes 4587520 | tf_op jit(solution)/shard_map/all_to_all | solution.py:55
  667.1 4.6 reshape.50
  (71 shorter events, 87.7 us)
Async XLA Ops:
  6.5 3.1 copy-start
  6.5 254.7 %all-gather.2.cloned.1.call-start = ((), (), s32[]{:S(2)}) async-start(), calls=%async_computation.2 | async-start | bytes 20643840 | tf_op jit(solution)/shard_map/all_gather | solution.py:46
  9.1 0.6 copy-start.2
  19.6 19.3 %collective-permute-start.14 = (bf16[1,10,7168]{2,1,0:T(8,128)(2,1)S(1)}, bf16[1,10,7168]{2,1,0:T(8,128)(2,1)S(1)}, u32[]{:S(2)}, u32[]{:S(2)}) collective-permute-start(bf16[1,10,7168]{2,1,0:T(8,128)(2,1)S(1)} %get-tuple-element.5), channel_id=1, source_target_pairs={{0,120},{8,112},{16,104},{24,96},{32,88},{40,80},{48,72},{56,64},{... | collective-permute-start | bytes 430088 | tf_op jit(solution)/shard_map/ppermute | solution.py:18
  26.1 17.1 %collective-permute-start.13 = (bf16[1,10,7168]{2,1,0:T(8,128)(2,1)S(1)}, bf16[1,10,7168]{2,1,0:T(8,128)(2,1)S(1)}, u32[]{:S(2)}, u32[]{:S(2)}) collective-permute-start(bf16[1,10,7168]{2,1,0:T(8,128)(2,1)S(1)} %get-tuple-element.6), channel_id=1, source_target_pairs={{0,112},{8,120},{16,96},{24,104},{32,80},{40,88},{48,64},{56,72},{... | collective-permute-start | bytes 430088 | tf_op jit(solution)/shard_map/ppermute | solution.py:18
  26.4 20.1 %collective-permute-start.12 = (bf16[1,10,7168]{2,1,0:T(8,128)(2,1)S(1)}, bf16[1,10,7168]{2,1,0:T(8,128)(2,1)S(1)}, u32[]{:S(2)}, u32[]{:S(2)}) collective-permute-start(bf16[1,10,7168]{2,1,0:T(8,128)(2,1)S(1)} %get-tuple-element.7), channel_id=1, source_target_pairs={{0,104},{8,96},{16,120},{24,112},{32,72},{40,64},{48,88},{56,80},{... | collective-permute-start | bytes 430088 | tf_op jit(solution)/shard_map/ppermute | solution.py:18
  29.3 37.0 %collective-permute-start.11 = (bf16[1,10,7168]{2,1,0:T(8,128)(2,1)S(1)}, bf16[1,10,7168]{2,1,0:T(8,128)(2,1)S(1)}, u32[]{:S(2)}, u32[]{:S(2)}) collective-permute-start(bf16[1,10,7168]{2,1,0:T(8,128)(2,1)S(1)} %get-tuple-element.8), channel_id=1, source_target_pairs={{0,96},{8,104},{16,112},{24,120},{32,64},{40,72},{48,80},{56,88},{... | collective-permute-start | bytes 430088 | tf_op jit(solution)/shard_map/ppermute | solution.py:18
  29.7 38.1 %collective-permute-start.10 = (bf16[1,10,7168]{2,1,0:T(8,128)(2,1)S(1)}, bf16[1,10,7168]{2,1,0:T(8,128)(2,1)S(1)}, u32[]{:S(2)}, u32[]{:S(2)}) collective-permute-start(bf16[1,10,7168]{2,1,0:T(8,128)(2,1)S(1)} %get-tuple-element.9), channel_id=1, source_target_pairs={{0,88},{8,80},{16,72},{24,64},{32,120},{40,112},{48,104},{56,96},{... | collective-permute-start | bytes 430088 | tf_op jit(solution)/shard_map/ppermute | solution.py:18
  38.9 30.6 %collective-permute-start.9 = (bf16[1,10,7168]{2,1,0:T(8,128)(2,1)S(1)}, bf16[1,10,7168]{2,1,0:T(8,128)(2,1)S(1)}, u32[]{:S(2)}, u32[]{:S(2)}) collective-permute-start(bf16[1,10,7168]{2,1,0:T(8,128)(2,1)S(1)} %get-tuple-element.10), channel_id=1, source_target_pairs={{0,80},{8,88},{16,64},{24,72},{32,112},{40,120},{48,96},{56,104},{... | collective-permute-start | bytes 430088 | tf_op jit(solution)/shard_map/ppermute | solution.py:18
  43.2 27.2 %collective-permute-start.8 = (bf16[1,10,7168]{2,1,0:T(8,128)(2,1)S(1)}, bf16[1,10,7168]{2,1,0:T(8,128)(2,1)S(1)}, u32[]{:S(2)}, u32[]{:S(2)}) collective-permute-start(bf16[1,10,7168]{2,1,0:T(8,128)(2,1)S(1)} %get-tuple-element.11), channel_id=1, source_target_pairs={{0,72},{8,64},{16,88},{24,80},{32,104},{40,96},{48,120},{56,112},{... | collective-permute-start | bytes 430088 | tf_op jit(solution)/shard_map/ppermute | solution.py:18
  46.5 26.3 %collective-permute-start.7 = (bf16[1,10,7168]{2,1,0:T(8,128)(2,1)S(1)}, bf16[1,10,7168]{2,1,0:T(8,128)(2,1)S(1)}, u32[]{:S(2)}, u32[]{:S(2)}) collective-permute-start(bf16[1,10,7168]{2,1,0:T(8,128)(2,1)S(1)} %get-tuple-element.12), channel_id=1, source_target_pairs={{0,64},{8,72},{16,80},{24,88},{32,96},{40,104},{48,112},{56,120},{... | collective-permute-start | bytes 430088 | tf_op jit(solution)/shard_map/ppermute | solution.py:18
  66.3 18.8 %collective-permute-start.6 = (bf16[1,10,7168]{2,1,0:T(8,128)(2,1)S(1)}, bf16[1,10,7168]{2,1,0:T(8,128)(2,1)S(1)}, u32[]{:S(2)}, u32[]{:S(2)}) collective-permute-start(bf16[1,10,7168]{2,1,0:T(8,128)(2,1)S(1)} %get-tuple-element.13), channel_id=1, source_target_pairs={{0,56},{8,48},{16,40},{24,32},{32,24},{40,16},{48,8},{56,0},{64,12... | collective-permute-start | bytes 430088 | tf_op jit(solution)/shard_map/ppermute | solution.py:18
  67.9 17.2 %collective-permute-start.5 = (bf16[1,10,7168]{2,1,0:T(8,128)(2,1)S(1)}, bf16[1,10,7168]{2,1,0:T(8,128)(2,1)S(1)}, u32[]{:S(2)}, u32[]{:S(2)}) collective-permute-start(bf16[1,10,7168]{2,1,0:T(8,128)(2,1)S(1)} %get-tuple-element.14), channel_id=1, source_target_pairs={{0,48},{8,56},{16,32},{24,40},{32,16},{40,24},{48,0},{56,8},{64,11... | collective-permute-start | bytes 430088 | tf_op jit(solution)/shard_map/ppermute | solution.py:18
  69.4 26.4 %collective-permute-start.4 = (bf16[1,10,7168]{2,1,0:T(8,128)(2,1)}, bf16[1,10,7168]{2,1,0:T(8,128)(2,1)S(1)}, u32[]{:S(2)}, u32[]{:S(2)}) collective-permute-start(bf16[1,10,7168]{2,1,0:T(8,128)(2,1)} %get-tuple-element.15), channel_id=1, source_target_pairs={{0,40},{8,32},{16,56},{24,48},{32,8},{40,0},{48,24},{56,16},{64,10... | collective-permute-start | bytes 430088 | tf_op jit(solution)/shard_map/ppermute | solution.py:18
  70.4 25.7 %collective-permute-start.3 = (bf16[1,10,7168]{2,1,0:T(8,128)(2,1)}, bf16[1,10,7168]{2,1,0:T(8,128)(2,1)}, u32[]{:S(2)}, u32[]{:S(2)}) collective-permute-start(bf16[1,10,7168]{2,1,0:T(8,128)(2,1)} %get-tuple-element.16), channel_id=1, source_target_pairs={{0,32},{8,40},{16,48},{24,56},{32,0},{40,8},{48,16},{56,24},{64,96... | collective-permute-start | bytes 430088 | tf_op jit(solution)/shard_map/ppermute | solution.py:18
  72.8 24.5 %collective-permute-start.2 = (bf16[1,10,7168]{2,1,0:T(8,128)(2,1)}, bf16[1,10,7168]{2,1,0:T(8,128)(2,1)}, u32[]{:S(2)}, u32[]{:S(2)}) collective-permute-start(bf16[1,10,7168]{2,1,0:T(8,128)(2,1)} %get-tuple-element.17), channel_id=1, source_target_pairs={{0,24},{8,16},{16,8},{24,0},{32,56},{40,48},{48,40},{56,32},{64,88... | collective-permute-start | bytes 430088 | tf_op jit(solution)/shard_map/ppermute | solution.py:18
  85.1 14.1 %collective-permute-start.1 = (bf16[1,10,7168]{2,1,0:T(8,128)(2,1)}, bf16[1,10,7168]{2,1,0:T(8,128)(2,1)}, u32[]{:S(2)}, u32[]{:S(2)}) collective-permute-start(bf16[1,10,7168]{2,1,0:T(8,128)(2,1)} %get-tuple-element.18), channel_id=1, source_target_pairs={{0,16},{8,24},{16,0},{24,8},{32,48},{40,56},{48,32},{56,40},{64,80... | collective-permute-start | bytes 430088 | tf_op jit(solution)/shard_map/ppermute | solution.py:18
  85.1 15.9 %collective-permute-start = (bf16[1,10,7168]{2,1,0:T(8,128)(2,1)}, bf16[1,10,7168]{2,1,0:T(8,128)(2,1)}, u32[]{:S(2)}, u32[]{:S(2)}) collective-permute-start(bf16[1,10,7168]{2,1,0:T(8,128)(2,1)} %get-tuple-element.19), channel_id=1, source_target_pairs={{0,8},{8,0},{16,24},{24,16},{32,40},{40,32},{48,56},{56,48},{64,72... | collective-permute-start | bytes 430088 | tf_op jit(solution)/shard_map/ppermute | solution.py:18
  667.1 4.6 copy-start.3
  667.1 4.6 copy-start.4
  667.1 8.2 %copy-start.1 = (bf16[128,7168]{1,0:T(8,128)(2,1)S(1)}, bf16[128,7168]{1,0:T(8,128)(2,1)}, u32[]{:S(2)}) copy-start(bf16[128,7168]{1,0:T(8,128)(2,1)} %param.6) | copy-start | bytes 5505028
Sparse Core Ops, SparseCore 0:
  169.5 91.6 all-gather.1
